TPU v7x, 32 devices: a whole 2x2x4 slice. The times are simulated.
32 devices in a mesh: seq: 4 (over z), shard: 8 (over y, x, core).
Axes of the slice: x: 2, y: 2, z: 4, core: 2. Of those that a mesh axis runs over, the one named last changes fastest.
Arguments:
- frames: bfloat16 [8, 1024, 1536], P('shard', 'seq'), may hold values from -6 to 6
- text_states: bfloat16 [8, 64, 1536], P('shard'), may hold values from -6 to 6
- norm_gain: bfloat16 [3, 1536], P(None, 'shard'), may hold values from 0.5 to 1.5
- norm_bias: bfloat16 [3, 1536], P(None, 'shard'), may hold values from -3 to 3
- self_project: bfloat16 [3, 1536, 1536], P(None, 'shard'), may hold values from -0.15625 to 0.15625
- self_output: bfloat16 [1536, 1536], P('shard'), may hold values from -1.75 to 1.75
- cross_project: bfloat16 [3, 1536, 1536], P(None, 'shard'), may hold values from -0.15625 to 0.15625
- cross_output: bfloat16 [1536, 1536], P('shard'), may hold values from -0.625 to 0.625
- up_weight: bfloat16 [1536, 6144], P('shard'), may hold values from -0.15625 to 0.15625
- down_weight: bfloat16 [6144, 1536], P('shard'), may hold values from -0.078125 to 0.078125
- cotangent: bfloat16 [8, 1024, 1536], P('shard', 'seq'), may hold values from -6 to 6
Outputs:
- output: bfloat16 [8, 1024, 1536], P('shard', 'seq')
- frames_grad: float32 [8, 1024, 1536], P('shard', 'seq')
- text_grad: float32 [8, 64, 1536], P('shard')
- gain_grad: float32 [3, 1536], P(None, 'shard')
- bias_grad: float32 [3, 1536], P(None, 'shard')
- self_project_grad: float32 [3, 1536, 1536], P(None, 'shard')
- self_output_grad: float32 [1536, 1536], P('shard')
- cross_project_grad: float32 [3, 1536, 1536], P(None, 'shard')
- cross_output_grad: float32 [1536, 1536], P('shard')
- up_grad: float32 [1536, 6144], P('shard')
- down_grad: float32 [6144, 1536], P('shard')
All inputs are finite; a program needn't handle non-finite values.
Results may differ from a plain program's by a relative error of at most 0.022.
Values may be sent and summed in bfloat16 or wider, within the bound.
No kernel may reach another device: no remote copies, remote signals or barrier semaphores. Data moves between devices by JAX's collectives and lax.ppermute only.
A program may use at most 384 MiB of HBM per device.

v0:
```python
import jax
import jax.numpy as jnp
from jax import lax
from jax.sharding import PartitionSpec as P

HEAD_DIM = 64
QBLOCK = 512
EPSILON = 1e-05
MASKED_SCORE = -1e30


def layer_norm(hidden, gain, shift):
    center = hidden - jnp.mean(hidden, axis=-1, keepdims=True)
    spread = lax.rsqrt(jnp.mean(center * center, axis=-1, keepdims=True) + EPSILON)
    return center * spread * gain + shift


def exact_gelu(values):
    return jax.nn.gelu(values, approximate=False)


def contract(form, left, right):
    return jnp.einsum(form, left, right, preferred_element_type=jnp.float32)


def split_heads(values):
    return values.reshape(values.shape[:-1] + (values.shape[-1] // HEAD_DIM, HEAD_DIM))


def join_heads(values):
    return values.reshape(values.shape[:-2] + (values.shape[-2] * values.shape[-1],))


def causal_visible(start_row, row_count, stop_row):
    row_place = start_row + lax.broadcasted_iota(jnp.int32, (row_count, stop_row), 0)
    column_place = lax.broadcasted_iota(jnp.int32, (row_count, stop_row), 1)
    return column_place <= row_place


def block_scores(queries, key_rows, start_row, stop_row, scaling):
    scores = (
        contract("cqhe,ckhe->chqk", queries[:, start_row:stop_row], key_rows[:, :stop_row])
        * scaling
    )
    return jnp.where(
        causal_visible(start_row, stop_row - start_row, stop_row), scores, MASKED_SCORE
    )


def self_forward(queries, key_rows, value_rows, scaling):
    length = queries.shape[1]
    outputs = []
    totals = []
    for start_row in range(0, length, QBLOCK):
        stop_row = start_row + QBLOCK
        scores = block_scores(queries, key_rows, start_row, stop_row, scaling)
        largest = jnp.max(scores, axis=-1, keepdims=True)
        weights = jnp.exp(scores - largest)
        summed = jnp.sum(weights, axis=-1, keepdims=True)
        shares = (weights / summed).astype(jnp.bfloat16)
        outputs.append(contract("chqk,ckhe->cqhe", shares, value_rows[:, :stop_row]))
        totals.append(largest + jnp.log(summed))
    return (jnp.concatenate(outputs, axis=1), totals)


def self_backward(queries, key_rows, value_rows, totals, grad_out, scaling):
    length = queries.shape[1]
    grad_queries = []
    grad_keys = jnp.zeros(key_rows.shape, jnp.float32)
    grad_values = jnp.zeros(value_rows.shape, jnp.float32)
    for number, start_row in enumerate(range(0, length, QBLOCK)):
        stop_row = start_row + QBLOCK
        query_block = queries[:, start_row:stop_row]
        grad_block = grad_out[:, start_row:stop_row]
        scores = block_scores(queries, key_rows, start_row, stop_row, scaling)
        shares = jnp.exp(scores - totals[number])
        grad_shares = contract("cqhe,ckhe->chqk", grad_block, value_rows[:, :stop_row])
        centred = jnp.sum(shares * grad_shares, axis=-1, keepdims=True)
        grad_scores = (shares * (grad_shares - centred)).astype(jnp.bfloat16)
        grad_queries.append(
            contract("chqk,ckhe->cqhe", grad_scores, key_rows[:, :stop_row]) * scaling
        )
        grad_keys = grad_keys.at[:, :stop_row].add(
            contract("chqk,cqhe->ckhe", grad_scores, query_block) * scaling
        )
        grad_values = grad_values.at[:, :stop_row].add(
            contract("chqk,cqhe->ckhe", shares.astype(jnp.bfloat16), grad_block)
        )
    return (jnp.concatenate(grad_queries, axis=1), grad_keys, grad_values)


def cross_softmax(queries, key_rows, scaling):
    scores = contract("cfhe,cxhe->chxf", queries, key_rows) * scaling
    largest = jnp.max(scores, axis=2, keepdims=True)
    weights = jnp.exp(scores - largest)
    return weights / jnp.sum(weights, axis=2, keepdims=True)


def fetch_self(self_project, self_output, norm_gain, norm_bias):
    return (
        lax.all_gather(self_project, "shard", axis=1, tiled=True),
        lax.all_gather(self_output, "shard", axis=0, tiled=True),
        lax.all_gather(norm_gain, "shard", axis=1, tiled=True),
        lax.all_gather(norm_bias, "shard", axis=1, tiled=True),
    )


def fetch_cross(cross_project, cross_output):
    return (
        lax.all_gather(cross_project, "shard", axis=1, tiled=True),
        lax.all_gather(cross_output, "shard", axis=0, tiled=True),
    )


def fetch_mlp(up_weight, down_weight):
    return (
        lax.all_gather(up_weight, "shard", axis=0, tiled=True),
        lax.all_gather(down_weight, "shard", axis=0, tiled=True),
    )


def body(
    frames,
    text_states,
    norm_gain,
    norm_bias,
    self_project,
    self_output,
    cross_project,
    cross_output,
    up_weight,
    down_weight,
    cotangent,
):
    scaling = HEAD_DIM ** (-0.5)
    project_all, output_all, gain_all, bias_all = fetch_self(
        self_project, self_output, norm_gain, norm_bias
    )
    gains = gain_all.astype(jnp.float32)
    biases = bias_all.astype(jnp.float32)
    hidden = frames.astype(jnp.float32)
    normed_one, norm_pull_one = jax.vjp(layer_norm, hidden, gains[0], biases[0])
    inputs_one = normed_one.astype(jnp.bfloat16)
    projected = contract("cfd,jde->jcfe", inputs_one, project_all).astype(jnp.bfloat16)
    by_heads = lax.all_to_all(projected, "seq", split_axis=3, concat_axis=2, tiled=True)
    queries = split_heads(by_heads[0])
    key_rows = split_heads(by_heads[1])
    value_rows = split_heads(by_heads[2])
    attended_heads, totals = self_forward(queries, key_rows, value_rows, scaling)
    attended = lax.all_to_all(
        join_heads(attended_heads).astype(jnp.bfloat16),
        "seq",
        split_axis=1,
        concat_axis=2,
        tiled=True,
    )
    hidden_one = hidden + contract("cfd,de->cfe", attended, output_all)
    cross_all, cross_out_all = fetch_cross(cross_project, cross_output)
    normed_two, norm_pull_two = jax.vjp(layer_norm, hidden_one, gains[1], biases[1])
    inputs_two = normed_two.astype(jnp.bfloat16)
    cross_queries = contract("cfd,de->cfe", inputs_two, cross_all[0]).astype(jnp.bfloat16)
    cross_pairs = contract("cxd,jde->jcxe", text_states, cross_all[1:]).astype(jnp.bfloat16)
    text_keys = split_heads(cross_pairs[0])
    text_values = split_heads(cross_pairs[1])
    cross_shares = cross_softmax(split_heads(cross_queries), text_keys, scaling)
    cross_low = cross_shares.astype(jnp.bfloat16)
    mixed_text = join_heads(contract("chxf,cxhe->cfhe", cross_low, text_values)).astype(
        jnp.bfloat16
    )
    hidden_two = hidden_one + contract("cfd,de->cfe", mixed_text, cross_out_all)
    up_all, down_all = fetch_mlp(up_weight, down_weight)
    normed_three, norm_pull_three = jax.vjp(layer_norm, hidden_two, gains[2], biases[2])
    inputs_three = normed_three.astype(jnp.bfloat16)
    before_act = contract("cfd,dk->cfk", inputs_three, up_all)
    activated, gelu_pull = jax.vjp(exact_gelu, before_act)
    activated_low = activated.astype(jnp.bfloat16)
    result = hidden_two + contract("cfk,kd->cfd", activated_low, down_all)
    output = result.astype(jnp.bfloat16)
    up_all, down_all = fetch_mlp(up_weight, down_weight)
    grad_result = cotangent.astype(jnp.float32)
    grad_down = contract("cfk,cfd->kd", activated_low, cotangent)
    grad_act = contract("cfd,kd->cfk", cotangent, down_all)
    grad_before = gelu_pull(grad_act)[0].astype(jnp.bfloat16)
    grad_up = contract("cfd,cfk->dk", inputs_three, grad_before)
    grad_inputs_three = contract("cfk,dk->cfd", grad_before, up_all)
    grad_two_part, gain_three, bias_three = norm_pull_three(grad_inputs_three)
    grad_hidden_two = grad_result + grad_two_part
    up_share, down_share = (
        lax.psum_scatter(
            grad_up.astype(jnp.bfloat16), "shard", scatter_dimension=0, tiled=True
        ).astype(jnp.float32),
        lax.psum_scatter(
            grad_down.astype(jnp.bfloat16), "shard", scatter_dimension=0, tiled=True
        ).astype(jnp.float32),
    )
    cross_all, cross_out_all = fetch_cross(cross_project, cross_output)
    grad_low_two = grad_hidden_two.astype(jnp.bfloat16)
    grad_cross_out = contract("cfd,cfe->de", mixed_text, grad_low_two)
    grad_mixed = split_heads(
        contract("cfe,de->cfd", grad_low_two, cross_out_all).astype(jnp.bfloat16)
    )
    grad_shares = contract("cfhe,cxhe->chxf", grad_mixed, text_values)
    centred = jnp.sum(cross_shares * grad_shares, axis=2, keepdims=True)
    grad_scores = (cross_shares * (grad_shares - centred)).astype(jnp.bfloat16)
    grad_cross_query = join_heads(
        contract("chxf,cxhe->cfhe", grad_scores, text_keys) * scaling
    ).astype(jnp.bfloat16)
    grad_text_keys = join_heads(
        contract("chxf,cfhe->cxhe", grad_scores, split_heads(cross_queries)) * scaling
    )
    grad_text_values = join_heads(contract("chxf,cfhe->cxhe", cross_low, grad_mixed))
    grad_pairs = lax.psum(jnp.stack([grad_text_keys, grad_text_values]).astype(jnp.bfloat16), "seq")
    grad_text = contract("jcxe,jde->cxd", grad_pairs, cross_all[1:])
    grad_cross_pairs = contract("cxd,jcxe->jde", text_states, grad_pairs)
    grad_cross_first = contract("cfd,cfe->de", inputs_two, grad_cross_query)
    grad_inputs_two = contract("cfe,de->cfd", grad_cross_query, cross_all[0])
    grad_one_part, gain_two, bias_two = norm_pull_two(grad_inputs_two)
    grad_hidden_one = grad_hidden_two + grad_one_part
    cross_stack = jnp.concatenate([grad_cross_first[None], grad_cross_pairs], axis=0)
    cross_share, cross_out_share = (
        lax.psum_scatter(
            cross_stack.astype(jnp.bfloat16), "shard", scatter_dimension=1, tiled=True
        ).astype(jnp.float32),
        lax.psum_scatter(
            grad_cross_out.astype(jnp.bfloat16), "shard", scatter_dimension=0, tiled=True
        ).astype(jnp.float32),
    )
    project_all, output_all, gain_all, bias_all = fetch_self(
        self_project, self_output, norm_gain, norm_bias
    )
    grad_low_one = grad_hidden_one.astype(jnp.bfloat16)
    grad_self_out = contract("cfd,cfe->de", attended, grad_low_one)
    grad_attended = contract("cfe,de->cfd", grad_low_one, output_all).astype(jnp.bfloat16)
    grad_heads = lax.all_to_all(grad_attended, "seq", split_axis=2, concat_axis=1, tiled=True)
    grad_queries, grad_keys, grad_values = self_backward(
        queries, key_rows, value_rows, totals, split_heads(grad_heads), scaling
    )
    grad_stacked = jnp.stack(
        [join_heads(grad_queries), join_heads(grad_keys), join_heads(grad_values)]
    ).astype(jnp.bfloat16)
    grad_projected = lax.all_to_all(grad_stacked, "seq", split_axis=2, concat_axis=3, tiled=True)
    grad_self_project = contract("cfd,jcfe->jde", inputs_one, grad_projected)
    grad_inputs_one = contract("jcfe,jde->cfd", grad_projected, project_all)
    grad_zero_part, gain_one, bias_one = norm_pull_one(grad_inputs_one)
    grad_frames = grad_hidden_one + grad_zero_part
    gain_stack = jnp.stack([gain_one, gain_two, gain_three])
    bias_stack = jnp.stack([bias_one, bias_two, bias_three])
    project_share, output_share, gain_share, bias_share = (
        lax.psum_scatter(
            grad_self_project.astype(jnp.bfloat16), "shard", scatter_dimension=1, tiled=True
        ).astype(jnp.float32),
        lax.psum_scatter(
            grad_self_out.astype(jnp.bfloat16), "shard", scatter_dimension=0, tiled=True
        ).astype(jnp.float32),
        lax.psum_scatter(
            gain_stack.astype(jnp.bfloat16), "shard", scatter_dimension=1, tiled=True
        ).astype(jnp.float32),
        lax.psum_scatter(
            bias_stack.astype(jnp.bfloat16), "shard", scatter_dimension=1, tiled=True
        ).astype(jnp.float32),
    )
    summed_parts = (
        lax.psum(project_share.astype(jnp.bfloat16), "seq").astype(jnp.float32),
        lax.psum(output_share.astype(jnp.bfloat16), "seq").astype(jnp.float32),
        lax.psum(cross_share[:1].astype(jnp.bfloat16), "seq").astype(jnp.float32),
        lax.psum(cross_out_share.astype(jnp.bfloat16), "seq").astype(jnp.float32),
        lax.psum(up_share.astype(jnp.bfloat16), "seq").astype(jnp.float32),
        lax.psum(down_share.astype(jnp.bfloat16), "seq").astype(jnp.float32),
        lax.psum(gain_share.astype(jnp.bfloat16), "seq").astype(jnp.float32),
        lax.psum(bias_share.astype(jnp.bfloat16), "seq").astype(jnp.float32),
    )
    cross_final = jnp.concatenate([summed_parts[2], cross_share[1:]], axis=0)
    return (
        output,
        grad_frames,
        grad_text,
        summed_parts[6],
        summed_parts[7],
        summed_parts[0],
        summed_parts[1],
        cross_final,
        summed_parts[3],
        summed_parts[4],
        summed_parts[5],
    )


def solution(mesh):
    return jax.shard_map(
        body,
        mesh=mesh,
        in_specs=(
            P("shard", "seq", None),
            P("shard", None, None),
            P(None, "shard"),
            P(None, "shard"),
            P(None, "shard", None),
            P("shard", None),
            P(None, "shard", None),
            P("shard", None),
            P("shard", None),
            P("shard", None),
            P("shard", "seq", None),
        ),
        out_specs=(
            P("shard", "seq", None),
            P("shard", "seq", None),
            P("shard", None, None),
            P(None, "shard"),
            P(None, "shard"),
            P(None, "shard", None),
            P("shard", None),
            P(None, "shard", None),
            P("shard", None),
            P("shard", None),
            P("shard", None),
        ),
        check_vma=False,
    )
```

profile of v0, /device:TPU:0, one launch (start us, length us, event | category | flops | bytes accessed | tf_op | source)
XLA Modules:
  0.0 1739.3 jit_solution(10451731953631284153)
XLA Ops:
  31.7 59.6 %all-gather.9.cloned.1.call-done = bf16[3,1536,1536]{2,1,0:T(8,128)(2,1)} async-done(((bf16[3,192,1536]{2,1,0:T(8,128)(2,1)}), bf16[3,1536,1536]{2,1,0:T(8,128)(2,1)}) %all-gather.9.cloned.1.call-update) | async-done | bytes 14155792 | tf_op jit(solution)/shard_map/all_gather | solution.py:101
  111.2 69.5 %all-to-all-done = bf16[3,1,256,1536]{2,0,1,3:T(4,128)(2,1)} async-done(((bf16[3,1,256,1536]{2,0,1,3:T(4,128)(2,1)}), bf16[3,1,256,1536]{2,0,1,3:T(4,128)(2,1)}, u32[]{:S(2)}, u32[]{:S(2)}) %all-to-all-start) | async-done | bytes 2359328 | tf_op jit(solution)/shard_map/all_to_all | solution.py:145
  228.0 11.9 all-to-all-done.1
  261.1 92.5 %all-gather.17.cloned.1.call-done = bf16[1536,6144]{1,0:T(8,128)(2,1)} async-done(((bf16[192,6144]{1,0:T(8,128)(2,1)}), bf16[1536,6144]{1,0:T(8,128)(2,1)}) %all-gather.17.cloned.1.call-update) | async-done | bytes 18874384 | tf_op jit(solution)/shard_map/all_gather | solution.py:117
  353.6 23.7 %multiply_convert_fusion.2 = (bf16[256,6144]{1,0:T(8,128)(2,1)}, f32[256,6144]{1,0:T(8,128)}, f32[256,6144]{1,0:T(8,128)}) fusion(bf16[1536,6144]{1,0:T(8,128)(2,1)} %all-gather.17.cloned.1.call-done, f32[1,256,1536]{2,1,0:T(8,128)S(1)} %get-tuple-element.192, f32[1536]{0:T(1024)S(1)} %get-tuple-element.161, f32[1536]{0:T(1024)S(1)} %get-tuple-element.206, ...), kind=kOutput, calls=%fused_computation.31 | convolution fusion | flops 4936040448 | bytes 36190208 | tf_op jit(solution)/shard_map/cfd,dk->cfk/dot_general | solution.py:23
  377.3 76.7 %all-gather.19.cloned.1.call-done = bf16[6144,1536]{1,0:T(8,128)(2,1)} async-done(((bf16[768,1536]{1,0:T(8,128)(2,1)}), bf16[6144,1536]{1,0:T(8,128)(2,1)}) %all-gather.19.cloned.1.call-update) | async-done | bytes 18874384 | tf_op jit(solution)/shard_map/all_gather | solution.py:118
  453.9 14.8 add_convert_fusion
  513.5 24.0 %all-reduce.7.cloned.1.call-done = bf16[2,64,1536]{2,1,0:T(8,128)(2,1)} async-done(((bf16[2,64,1536]{2,1,0:T(8,128)(2,1)}), bf16[2,64,1536]{2,1,0:T(8,128)(2,1)}) %all-reduce.7.cloned.1.call-update) | async-done | bytes 393232 | tf_op jit(solution)/shard_map/psum | solution.py:212
  547.7 30.8 %copy.225 = bf16[3,1536,1536]{2,0,1:T(4,128)(2,1)} copy(bf16[3,1536,1536]{1,2,0:T(8,128)(2,1)} %pad_maximum_fusion) | data formatting | bytes 28311552
  578.5 17.0 copy.233
  620.5 18.2 %all-to-all-done.2 = bf16[4,2,49152]{2,1,0:T(2,128)(2,1)S(1)} async-done(((bf16[4,2,49152]{2,1,0:T(2,128)(2,1)}), bf16[4,2,49152]{2,1,0:T(2,128)(2,1)S(1)}, u32[]{:S(2)}, u32[]{:S(2)}) %all-to-all-start.2) | async-done | bytes 786464 | tf_op jit(solution)/shard_map/all_to_all | solution.py:234
  709.7 72.8 %all_to_all.60 = bf16[3,1,1024,384]{3,0,1,2:T(4,128)(2,1)S(1)} all-to-all(bf16[3,1,1024,384]{3,0,1,2:T(4,128)(2,1)S(1)} %pad_maximum_fusion.1), channel_id=1, replica_groups=mesh['seq'=4,'shard'=8] {'seq'}, dimensions={2} | all-to-all | bytes 4718592 | tf_op jit(solution)/shard_map/all_to_all | solution.py:241
  797.7 30.8 %copy.223 = bf16[3,1536,1536]{2,0,1:T(4,128)(2,1)} copy(bf16[3,1536,1536]{1,2,0:T(8,128)(2,1)} %convert_bitcast_fusion) | data formatting | bytes 28311552
  828.6 17.0 copy.232
  858.2 12.6 convolution_convert_fusion.1
  906.5 40.3 %reduce-scatter.29.cloned.1.call-done = bf16[192,4608]{1,0:T(8,128)(2,1)} async-done(((bf16[1536,4608]{1,0:T(8,128)(2,1)}), bf16[192,4608]{1,0:T(8,128)(2,1)}) %reduce-scatter.29.cloned.1.call-update) | async-done | bytes 1769488
  957.5 46.9 %reduce-scatter.19.cloned.1.call-done = bf16[192,1536]{1,0:T(8,128)(2,1)} async-done(((bf16[1536,1536]{1,0:T(8,128)(2,1)}), bf16[192,1536]{1,0:T(8,128)(2,1)}) %reduce-scatter.19.cloned.1.call-update) | async-done | bytes 589840 | tf_op jit(solution)/shard_map/reduce_scatter | solution.py:224
  1004.5 57.8 %reduce-scatter.17.cloned.1.call-done = bf16[192,1536]{1,0:T(8,128)(2,1)} async-done(((bf16[1536,1536]{1,0:T(8,128)(2,1)}), bf16[192,1536]{1,0:T(8,128)(2,1)}) %reduce-scatter.17.cloned.1.call-update) | async-done | bytes 589840 | tf_op jit(solution)/shard_map/reduce_scatter | solution.py:252
  1062.3 129.9 %reduce-scatter.21.cloned.1.call-done = bf16[192,6144]{1,0:T(8,128)(2,1)} async-done(((bf16[1536,6144]{1,0:T(8,128)(2,1)}), bf16[192,6144]{1,0:T(8,128)(2,1)}) %reduce-scatter.21.cloned.1.call-update) | async-done | bytes 2359312 | tf_op jit(solution)/shard_map/reduce_scatter | solution.py:189
  1192.2 130.1 %reduce-scatter.23.cloned.1.call-done = bf16[768,1536]{1,0:T(8,128)(2,1)} async-done(((bf16[6144,1536]{1,0:T(8,128)(2,1)}), bf16[768,1536]{1,0:T(8,128)(2,1)}) %reduce-scatter.23.cloned.1.call-update) | async-done | bytes 2359312 | tf_op jit(solution)/shard_map/reduce_scatter | solution.py:192
  1343.7 15.4 reduce-scatter.25.cloned.1.call-done
  1360.0 35.9 %reduce-scatter.27.cloned.1.call-done = bf16[192,3]{1,0:T(8,128)(2,1)} async-done(((bf16[1536,3]{1,0:T(8,128)(2,1)}), bf16[192,3]{1,0:T(8,128)(2,1)}) %reduce-scatter.27.cloned.1.call-update) | async-done | bytes 1168
  1396.8 11.9 all-reduce.2
  1414.7 297.1 %all-reduce.9.cloned.1.call-done = (bf16[3,192,1536]{1,2,0:T(8,128)(2,1)}, bf16[192,1536]{1,0:T(8,128)(2,1)}, bf16[1,192,1536]{1,2,0:T(8,128)(2,1)}, bf16[192,15...) async-done(((bf16[3,192,1536]{1,2,0:T(8,128)(2,1)}, bf16[192,1536]{1,0:T(8,128)(2,1)}, bf16[1,192,1536]{1,2,0:T(8,128)(2,1)}, ...) | async-done | bytes 8257552 | tf_op jit(solution)/shard_map/psum | solution.py:263
  (380 shorter events, 386.4 us)
Async XLA Ops:
  7.2 84.2 %all-gather.9.cloned.1.call-start = ((), (), s32[]{:S(2)}) async-start(), calls=%async_computation.12 | async-start | bytes 15925248 | tf_op jit(solution)/shard_map/all_gather | solution.py:101
  7.9 212.1 %all-gather.13.cloned.1.call-start = ((), (), s32[]{:S(2)}) async-start(), calls=%async_computation.14 | async-start | bytes 15925248 | tf_op jit(solution)/shard_map/all_gather | solution.py:110
  8.7 232.6 %all-gather.11.cloned.1.call-start = ((), (), s32[]{:S(2)}) async-start(), calls=%async_computation.13 | async-start | bytes 5308416 | tf_op jit(solution)/shard_map/all_gather | solution.py:102
  9.4 247.2 %all-gather.15.cloned.1.call-start = ((), (), s32[]{:S(2)}) async-start(), calls=%async_computation.15 | async-start | bytes 5308416 | tf_op jit(solution)/shard_map/all_gather | solution.py:111
  10.0 343.6 %all-gather.17.cloned.1.call-start = ((), (), s32[]{:S(2)}) async-start(), calls=%async_computation.16 | async-start | bytes 21233664 | tf_op jit(solution)/shard_map/all_gather | solution.py:117
  10.6 443.3 %all-gather.19.cloned.1.call-start = ((), (), s32[]{:S(2)}) async-start(), calls=%async_computation.17 | async-start | bytes 21233664 | tf_op jit(solution)/shard_map/all_gather | solution.py:118
  31.1 214.7 %copy-start.67 = (f32[1536]{0:T(1024)}, f32[1536]{0:T(1024)S(1)}, u32[]{:S(2)}) copy-start(f32[1536]{0:T(1024)S(1)} %get-tuple-element.205) | copy-start | bytes 18436
  31.1 214.7 %copy-start.83 = (f32[1536]{0:T(1024)}, f32[1536]{0:T(1024)S(1)}, u32[]{:S(2)}) copy-start(f32[1536]{0:T(1024)S(1)} %get-tuple-element.162) | copy-start | bytes 18436
  31.1 322.4 %copy-start.56 = (f32[1536]{0:T(1024)}, f32[1536]{0:T(1024)S(1)}, u32[]{:S(2)}) copy-start(f32[1536]{0:T(1024)S(1)} %get-tuple-element.161) | copy-start | bytes 18436
  104.3 76.4 %all-to-all-start = ((bf16[3,1,256,1536]{2,0,1,3:T(4,128)(2,1)}), bf16[3,1,256,1536]{2,0,1,3:T(4,128)(2,1)}, u32[]{:S(2)}, u32[]{:S(2)}) async-start(bf16[3,1,256,1536]{2,0,1,3:T(4,128)(2,1)} %copy.187), calls=%async_computation | async-start | bytes 6291456 | tf_op jit(solution)/shard_map/all_to_all | solution.py:145
  216.4 23.5 %all-to-all-start.1 = ((bf16[4,2,49152]{2,1,0:T(2,128)(2,1)}), bf16[4,2,49152]{2,1,0:T(2,128)(2,1)S(1)}, u32[]{:S(2)}, u32[]{:S(2)}) async-start(bf16[4,2,49152]{2,1,0:T(2,128)(2,1)} %reshape.954), calls=%async_computation.1 | async-start | bytes 1572864 | tf_op jit(solution)/shard_map/all_to_all | solution.py:150
  220.0 317.6 %all-reduce.7.cloned.1.call-start = ((), (), s32[]{:S(2)}) async-start(), calls=%async_computation.18 | async-start | bytes 786432 | tf_op jit(solution)/shard_map/psum | solution.py:212
  254.0 237.8 %copy-start.58 = (f32[24,256]{1,0:T(8,128)}, f32[24,256]{1,0:T(8,128)S(1)}, u32[]{:S(2)}) copy-start(f32[24,256]{1,0:T(8,128)S(1)} %get-tuple-element.189) | copy-start | bytes 73732
  260.8 218.7 %copy-start.9 = (f32[1,256,1536]{2,1,0:T(8,128)}, f32[1,256,1536]{2,1,0:T(8,128)S(1)}, u32[]{:S(2)}) copy-start(f32[1,256,1536]{2,1,0:T(8,128)S(1)} %get-tuple-element.192) | copy-start | bytes 4718596
  500.4 396.8 %reduce-scatter.31.cloned.1.call-start = ((), (), s32[]{:S(2)}) async-start(), calls=%async_computation.26 | async-start | bytes 15925248
  616.7 22.0 %all-to-all-start.2 = ((bf16[4,2,49152]{2,1,0:T(2,128)(2,1)}), bf16[4,2,49152]{2,1,0:T(2,128)(2,1)S(1)}, u32[]{:S(2)}, u32[]{:S(2)}) async-start(bf16[4,2,49152]{2,1,0:T(2,128)(2,1)} %reshape.956), calls=%async_computation.2 | async-start | bytes 1572864 | tf_op jit(solution)/shard_map/all_to_all | solution.py:234
  620.5 326.3 %reduce-scatter.29.cloned.1.call-start = ((), (), s32[]{:S(2)}) async-start(), calls=%async_computation.25 | async-start | bytes 15925248
  845.6 158.8 %reduce-scatter.19.cloned.1.call-start = ((), (), s32[]{:S(2)}) async-start(), calls=%async_computation.20 | async-start | bytes 5308416 | tf_op jit(solution)/shard_map/reduce_scatter | solution.py:224
  851.5 210.8 %reduce-scatter.17.cloned.1.call-start = ((), (), s32[]{:S(2)}) async-start(), calls=%async_computation.19 | async-start | bytes 5308416 | tf_op jit(solution)/shard_map/reduce_scatter | solution.py:252
  857.6 334.7 %reduce-scatter.21.cloned.1.call-start = ((), (), s32[]{:S(2)}) async-start(), calls=%async_computation.21 | async-start | bytes 21233664 | tf_op jit(solution)/shard_map/reduce_scatter | solution.py:189
  870.8 451.5 %reduce-scatter.23.cloned.1.call-start = ((), (), s32[]{:S(2)}) async-start(), calls=%async_computation.22 | async-start | bytes 21233664 | tf_op jit(solution)/shard_map/reduce_scatter | solution.py:192
  882.3 476.8 %reduce-scatter.25.cloned.1.call-start = ((), (), s32[]{:S(2)}) async-start(), calls=%async_computation.23 | async-start | bytes 442368
  895.9 500.1 %reduce-scatter.27.cloned.1.call-start = ((), (), s32[]{:S(2)}) async-start(), calls=%async_computation.24 | async-start | bytes 442368
  897.0 814.8 %all-reduce.9.cloned.1.call-start = ((), (), s32[]{:S(2)}) async-start(), calls=%async_computation.27 | async-start | bytes 18087936 | tf_op jit(solution)/shard_map/psum | solution.py:263
  (91 other events, 1119.1 us)
Sparse Core Ops, SparseCore 0:
  9.9 81.4 all-gather.8
  93.3 78.6 all-gather.12
  173.8 38.7 all-gather.10
  214.4 38.7 all-gather.14
  255.0 98.5 all-gather.16
  355.3 98.5 all-gather.18
  500.6 36.9 all-reduce.6
  595.7 101.5 reduce-scatter.30
  845.8 100.9 reduce-scatter.28
  950.6 53.7 reduce-scatter.18
  1008.5 53.7 reduce-scatter.16
  1065.8 126.4 reduce-scatter.20
  1195.8 126.4 reduce-scatter.22
  1325.2 33.8 reduce-scatter.24
  1362.0 33.8 reduce-scatter.26
  1399.6 312.1 all-reduce.8
where the time goes:
time: 1750 us; the launch traced here: 1740 us
  waiting for transfers between devices  1110 us (63%)
  matrix products  220 us (13%)
  local copies, waits for them, and re-layouts  207 us (12%)
  blocking collectives  104 us (6%)
  other arithmetic  70.1 us (4%)
    psum x1, waiting for transfers between devices, body(): lax.psum(project_share.astype(jnp.bfloat16), 'seq').astype(jnp.float32)  297 us
    dot_general x38, matrix products, contract(): return jnp.einsum(form, left, right, preferred_element_type=jnp.float32)  218 us
    unnamed x214, local copies, waits for them, and re-layouts  146 us
    reduce_scatter x1, waiting for transfers between devices, body(): lax.psum_scatter(grad_down.astype(jnp.bfloat16), 'shard', scatter_dimensi...  130 us
    reduce_scatter x1, waiting for transfers between devices, body(): lax.psum_scatter(grad_up.astype(jnp.bfloat16), 'shard', scatter_dimension...  130 us
    unnamed x20, waiting for transfers between devices  95.5 us
    all_gather x1, waiting for transfers between devices, fetch_mlp(): lax.all_gather(up_weight, 'shard', axis=0, tiled=True)  92.5 us
    all_gather x1, waiting for transfers between devices, fetch_mlp(): lax.all_gather(down_weight, 'shard', axis=0, tiled=True)  76.7 us
  transfers between devices with their start and end apart: 19, of which 15 were waited for; matrix products, arithmetic and copies ran while one was open for 21% of the time, Pallas kernels for 0%

commit v1 on v0

--- a/solution.py
+++ b/solution.py
@@ -260,7 +260,9 @@
         ).astype(jnp.float32),
     )
     summed_parts = (
-        lax.psum(project_share.astype(jnp.bfloat16), "seq").astype(jnp.float32),
+        jnp.sum(lax.all_gather(project_share.astype(jnp.bfloat16), "seq"), axis=0).astype(
+            jnp.float32
+        ),
         lax.psum(output_share.astype(jnp.bfloat16), "seq").astype(jnp.float32),
         lax.psum(cross_share[:1].astype(jnp.bfloat16), "seq").astype(jnp.float32),
         lax.psum(cross_out_share.astype(jnp.bfloat16), "seq").astype(jnp.float32),

time: 1750 us -> 1650 us (0.943)
  waiting for transfers between devices: 1110 us -> 995 us
    all_gather x0 -> x1, waiting for transfers between devices: none -> 110 us  [body(): lax.all_gather(project_share.astype(jnp.bfloat16), 'seq')]
    reduce_scatter x1, waiting for transfers between devices: 130 us -> 29.4 us  [body(): lax.psum_scatter(grad_up.astype(jnp.bfloat16), 'shard', scatter_dimension...]
    psum x1, waiting for transfers between devices: 297 us -> 220 us  [body(): lax.psum(output_share.astype(jnp.bfloat16), 'seq').astype(jnp.float32)]
    reduce_scatter x1, waiting for transfers between devices: 57.8 us -> 0.01 us  [body(): lax.psum_scatter(grad_self_out.astype(jnp.bfloat16), 'shard', scatter_dim...]
    unnamed x20 -> x21, waiting for transfers between devices: 95.5 us -> 153 us
    reduce_scatter x1, waiting for transfers between devices: 46.9 us -> 0.01 us  [body(): lax.psum_scatter(grad_cross_out.astype(jnp.bfloat16), 'shard', scatter_di...]
    unnamed x214 -> x202, local copies, waits for them, and re-layouts: 146 us -> 144 us
  transfers between devices with their start and end apart: 19 -> 20, of which waited for: 15 -> 14; matrix products, arithmetic and copies ran while one was open for 21% -> 23% of each run, Pallas kernels for 0% -> 0%
where the time goes in v1:
time: 1650 us; the launch traced here: 1640 us
  waiting for transfers between devices  995 us (60%)
  matrix products  225 us (14%)
  local copies, waits for them, and re-layouts  207 us (13%)
  blocking collectives  105 us (6%)
  other arithmetic  78.6 us (5%)
    dot_general x38, matrix products, contract(): return jnp.einsum(form, left, right, preferred_element_type=jnp.float32)  223 us
    psum x1, waiting for transfers between devices, body(): lax.psum(output_share.astype(jnp.bfloat16), 'seq').astype(jnp.float32)  220 us
    unnamed x21, waiting for transfers between devices  153 us
    unnamed x202, local copies, waits for them, and re-layouts  144 us
    reduce_scatter x1, waiting for transfers between devices, body(): lax.psum_scatter(grad_down.astype(jnp.bfloat16), 'shard', scatter_dimensi...  130 us
    all_gather x1, waiting for transfers between devices, body(): lax.all_gather(project_share.astype(jnp.bfloat16), 'seq')  110 us
    all_gather x1, waiting for transfers between devices, fetch_mlp(): lax.all_gather(up_weight, 'shard', axis=0, tiled=True)  93.7 us
    all_gather x1, waiting for transfers between devices, fetch_mlp(): lax.all_gather(down_weight, 'shard', axis=0, tiled=True)  76.6 us
  transfers between devices with their start and end apart: 20, of which 14 were waited for; matrix products, arithmetic and copies ran while one was open for 23% of the time, Pallas kernels for 0%

profile of v1, /device:TPU:0, one launch (start us, length us, event | category | flops | bytes accessed | tf_op | source)
XLA Modules:
  0.0 1640.1 jit_solution(5969772384294088082)
XLA Ops:
  31.7 59.6 %all-gather.11.cloned.1.call-done = bf16[3,1536,1536]{2,1,0:T(8,128)(2,1)} async-done(((bf16[3,192,1536]{2,1,0:T(8,128)(2,1)}), bf16[3,1536,1536]{2,1,0:T(8,128)(2,1)}) %all-gather.11.cloned.1.call-update) | async-done | bytes 14155792 | tf_op jit(solution)/shard_map/all_gather | solution.py:101
  111.4 69.5 %all-to-all-done = bf16[3,1,256,1536]{2,0,1,3:T(4,128)(2,1)} async-done(((bf16[3,1,256,1536]{2,0,1,3:T(4,128)(2,1)}), bf16[3,1,256,1536]{2,0,1,3:T(4,128)(2,1)}, u32[]{:S(2)}, u32[]{:S(2)}) %all-to-all-start) | async-done | bytes 2359328 | tf_op jit(solution)/shard_map/all_to_all | solution.py:145
  228.0 11.8 all-to-all-done.1
  259.9 93.7 %all-gather.19.cloned.1.call-done = bf16[1536,6144]{1,0:T(8,128)(2,1)} async-done(((bf16[192,6144]{1,0:T(8,128)(2,1)}), bf16[1536,6144]{1,0:T(8,128)(2,1)}) %all-gather.19.cloned.1.call-update) | async-done | bytes 18874384 | tf_op jit(solution)/shard_map/all_gather | solution.py:117
  353.6 23.7 %multiply_convert_fusion.2 = (bf16[256,6144]{1,0:T(8,128)(2,1)}, f32[256,6144]{1,0:T(8,128)}, f32[256,6144]{1,0:T(8,128)}) fusion(bf16[1536,6144]{1,0:T(8,128)(2,1)} %all-gather.19.cloned.1.call-done, f32[1,256,1536]{2,1,0:T(8,128)S(1)} %get-tuple-element.191, f32[1536]{0:T(1024)S(1)} %get-tuple-element.161, f32[1536]{0:T(1024)S(1)} %get-tuple-element.205, ...), kind=kOutput, calls=%fused_computation.31 | convolution fusion | flops 4936040448 | bytes 36190208 | tf_op jit(solution)/shard_map/cfd,dk->cfk/dot_general | solution.py:23
  377.3 76.6 %all-gather.21.cloned.1.call-done = bf16[6144,1536]{1,0:T(8,128)(2,1)} async-done(((bf16[768,1536]{1,0:T(8,128)(2,1)}), bf16[6144,1536]{1,0:T(8,128)(2,1)}) %all-gather.21.cloned.1.call-update) | async-done | bytes 18874384 | tf_op jit(solution)/shard_map/all_gather | solution.py:118
  453.9 15.3 add_convert_fusion
  517.6 22.6 %all-reduce.7.cloned.1.call-done = bf16[2,64,1536]{2,1,0:T(8,128)(2,1)} async-done(((bf16[2,64,1536]{2,1,0:T(8,128)(2,1)}), bf16[2,64,1536]{2,1,0:T(8,128)(2,1)}) %all-reduce.7.cloned.1.call-update) | async-done | bytes 393232 | tf_op jit(solution)/shard_map/psum | solution.py:212
  550.3 31.0 %copy.230 = bf16[3,1536,1536]{2,0,1:T(4,128)(2,1)} copy(bf16[3,1536,1536]{1,2,0:T(8,128)(2,1)} %pad_maximum_fusion) | data formatting | bytes 28311552
  581.3 17.0 %copy.240 = bf16[192,8,3,1536]{3,1,2,0:T(8,128)(2,1)} copy(bf16[192,8,3,1536]{3,2,1,0:T(4,128)(2,1)} %bitcast.329) | data formatting | bytes 28311552
  617.2 11.8 convolution_convert_fusion.1
  629.1 12.5 convolution_convert_fusion
  662.1 18.7 %all-to-all-done.2 = bf16[4,2,49152]{2,1,0:T(2,128)(2,1)S(1)} async-done(((bf16[4,2,49152]{2,1,0:T(2,128)(2,1)}), bf16[4,2,49152]{2,1,0:T(2,128)(2,1)S(1)}, u32[]{:S(2)}, u32[]{:S(2)}) %all-to-all-start.2) | async-done | bytes 786464 | tf_op jit(solution)/shard_map/all_to_all | solution.py:234
  752.0 73.0 %all_to_all.60 = bf16[3,1,1024,384]{3,0,1,2:T(4,128)(2,1)S(1)} all-to-all(bf16[3,1,1024,384]{3,0,1,2:T(4,128)(2,1)S(1)} %pad_maximum_fusion.1), channel_id=1, replica_groups=mesh['seq'=4,'shard'=8] {'seq'}, dimensions={2} | all-to-all | bytes 4718592 | tf_op jit(solution)/shard_map/all_to_all | solution.py:241
  842.8 31.5 %copy.228 = bf16[3,1536,1536]{2,0,1:T(4,128)(2,1)} copy(bf16[3,1536,1536]{1,2,0:T(8,128)(2,1)} %convert_bitcast_fusion) | data formatting | bytes 28311552
  874.2 17.4 %copy.239 = bf16[192,8,3,1536]{3,1,2,0:T(8,128)(2,1)} copy(bf16[192,8,3,1536]{3,2,1,0:T(4,128)(2,1)} %bitcast.330) | data formatting | bytes 28311552
  916.2 29.4 %reduce-scatter.21.cloned.1.call-done = bf16[192,6144]{1,0:T(8,128)(2,1)} async-done(((bf16[1536,6144]{1,0:T(8,128)(2,1)}), bf16[192,6144]{1,0:T(8,128)(2,1)}) %reduce-scatter.21.cloned.1.call-update) | async-done | bytes 2359312 | tf_op jit(solution)/shard_map/reduce_scatter | solution.py:189
  945.7 129.9 %reduce-scatter.23.cloned.1.call-done = bf16[768,1536]{1,0:T(8,128)(2,1)} async-done(((bf16[6144,1536]{1,0:T(8,128)(2,1)}), bf16[768,1536]{1,0:T(8,128)(2,1)}) %reduce-scatter.23.cloned.1.call-update) | async-done | bytes 2359312 | tf_op jit(solution)/shard_map/reduce_scatter | solution.py:192
  1075.7 105.3 %reduce-scatter.29.cloned.1.call-done = bf16[192,4608]{1,0:T(8,128)(2,1)} async-done(((bf16[1536,4608]{1,0:T(8,128)(2,1)}), bf16[192,4608]{1,0:T(8,128)(2,1)}) %reduce-scatter.29.cloned.1.call-update) | async-done | bytes 1769488
  1189.6 10.9 fusion.31
  1218.7 35.9 %reduce-scatter.27.cloned.1.call-done = bf16[192,3]{1,0:T(8,128)(2,1)} async-done(((bf16[1536,3]{1,0:T(8,128)(2,1)}), bf16[192,3]{1,0:T(8,128)(2,1)}) %reduce-scatter.27.cloned.1.call-update) | async-done | bytes 1168
  1255.5 12.0 all-reduce.2
  1273.5 220.0 %all-reduce.9.cloned.1.call-done = (bf16[192,1536]{1,0:T(8,128)(2,1)}, bf16[1,192,1536]{1,2,0:T(8,128)(2,1)}, bf16[192,1536]{1,0:T(8,128)(2,1)}, bf16[192,6144]{1,0:T(8,128)(2,1)}, bf16[768,1536]{1,0:T(8,128)(2,1)}) async-done(((bf16[192,1536]{1,0:T(8,128)(2,1)}, bf16[1,192,1536]{1,2,0:T(8,128)(2,1)}, bf16[192,1536]{1,0:T(8,128)(2,1)}, bf16[192,6144]{1,0:T(8,128)(2,1)}, bf16[768,1536]{1,0:T(8,128)(2,1)}), ...) | async-done | bytes 6488080 | tf_op jit(solution)/shard_map/psum | solution.py:266
  1512.5 109.6 %all-gather.23.cloned.1.call-done = bf16[12,192,1536]{2,1,0:T(8,128)(2,1)} async-done(((bf16[3,192,1536]{2,1,0:T(8,128)(2,1)}), bf16[12,192,1536]{2,1,0:T(8,128)(2,1)}) %all-gather.23.cloned.1.call-update) | async-done | bytes 7077904 | tf_op jit(solution)/shard_map/all_gather | solution.py:263
  (372 shorter events, 385.8 us)
Async XLA Ops:
  7.2 84.2 %all-gather.11.cloned.1.call-start = ((), (), s32[]{:S(2)}) async-start(), calls=%async_computation.12 | async-start | bytes 15925248 | tf_op jit(solution)/shard_map/all_gather | solution.py:101
  7.9 212.1 %all-gather.15.cloned.1.call-start = ((), (), s32[]{:S(2)}) async-start(), calls=%async_computation.14 | async-start | bytes 15925248 | tf_op jit(solution)/shard_map/all_gather | solution.py:110
  8.7 232.5 %all-gather.13.cloned.1.call-start = ((), (), s32[]{:S(2)}) async-start(), calls=%async_computation.13 | async-start | bytes 5308416 | tf_op jit(solution)/shard_map/all_gather | solution.py:102
  9.4 245.5 %all-gather.17.cloned.1.call-start = ((), (), s32[]{:S(2)}) async-start(), calls=%async_computation.15 | async-start | bytes 5308416 | tf_op jit(solution)/shard_map/all_gather | solution.py:111
  10.0 343.6 %all-gather.19.cloned.1.call-start = ((), (), s32[]{:S(2)}) async-start(), calls=%async_computation.16 | async-start | bytes 21233664 | tf_op jit(solution)/shard_map/all_gather | solution.py:117
  10.6 443.3 %all-gather.21.cloned.1.call-start = ((), (), s32[]{:S(2)}) async-start(), calls=%async_computation.17 | async-start | bytes 21233664 | tf_op jit(solution)/shard_map/all_gather | solution.py:118
  104.3 76.6 %all-to-all-start = ((bf16[3,1,256,1536]{2,0,1,3:T(4,128)(2,1)}), bf16[3,1,256,1536]{2,0,1,3:T(4,128)(2,1)}, u32[]{:S(2)}, u32[]{:S(2)}) async-start(bf16[3,1,256,1536]{2,0,1,3:T(4,128)(2,1)} %copy.190), calls=%async_computation | async-start | bytes 6291456 | tf_op jit(solution)/shard_map/all_to_all | solution.py:145
  216.4 23.4 %all-to-all-start.1 = ((bf16[4,2,49152]{2,1,0:T(2,128)(2,1)}), bf16[4,2,49152]{2,1,0:T(2,128)(2,1)S(1)}, u32[]{:S(2)}, u32[]{:S(2)}) async-start(bf16[4,2,49152]{2,1,0:T(2,128)(2,1)} %reshape.955), calls=%async_computation.1 | async-start | bytes 1572864 | tf_op jit(solution)/shard_map/all_to_all | solution.py:150
  219.9 320.2 %all-reduce.7.cloned.1.call-start = ((), (), s32[]{:S(2)}) async-start(), calls=%async_computation.18 | async-start | bytes 786432 | tf_op jit(solution)/shard_map/psum | solution.py:212
  252.4 240.4 %copy-start.54 = (f32[24,256]{1,0:T(8,128)}, f32[24,256]{1,0:T(8,128)S(1)}, u32[]{:S(2)}) copy-start(f32[24,256]{1,0:T(8,128)S(1)} %get-tuple-element.188) | copy-start | bytes 73732
  259.5 357.1 %copy-start.8 = (f32[1,256,1536]{2,1,0:T(8,128)}, f32[1,256,1536]{2,1,0:T(8,128)S(1)}, u32[]{:S(2)}) copy-start(f32[1,256,1536]{2,1,0:T(8,128)S(1)} %get-tuple-element.191) | copy-start | bytes 4718596
  259.5 220.4 %copy-start.61 = (f32[256]{0:T(256)}, f32[256]{0:T(256)S(1)}, u32[]{:S(2)}) copy-start(f32[256]{0:T(256)S(1)} %broadcast_multiply_fusion) | copy-start | bytes 3076
  259.9 220.1 %copy-start.71 = (f32[256]{0:T(256)}, f32[256]{0:T(256)S(1)}, u32[]{:S(2)}) copy-start(f32[256]{0:T(256)S(1)} %fusion.102) | copy-start | bytes 3076
  503.0 404.0 %reduce-scatter.31.cloned.1.call-start = ((), (), s32[]{:S(2)}) async-start(), calls=%async_computation.27 | async-start | bytes 15925248
  598.3 317.9 %reduce-scatter.19.cloned.1.call-start = ((), (), s32[]{:S(2)}) async-start(), calls=%async_computation.20 | async-start | bytes 5308416 | tf_op jit(solution)/shard_map/reduce_scatter | solution.py:224
  603.4 312.9 %reduce-scatter.17.cloned.1.call-start = ((), (), s32[]{:S(2)}) async-start(), calls=%async_computation.19 | async-start | bytes 5308416 | tf_op jit(solution)/shard_map/reduce_scatter | solution.py:252
  616.6 329.1 %reduce-scatter.21.cloned.1.call-start = ((), (), s32[]{:S(2)}) async-start(), calls=%async_computation.21 | async-start | bytes 21233664 | tf_op jit(solution)/shard_map/reduce_scatter | solution.py:189
  629.0 446.6 %reduce-scatter.23.cloned.1.call-start = ((), (), s32[]{:S(2)}) async-start(), calls=%async_computation.22 | async-start | bytes 21233664 | tf_op jit(solution)/shard_map/reduce_scatter | solution.py:192
  657.4 23.4 %all-to-all-start.2 = ((bf16[4,2,49152]{2,1,0:T(2,128)(2,1)}), bf16[4,2,49152]{2,1,0:T(2,128)(2,1)S(1)}, u32[]{:S(2)}, u32[]{:S(2)}) async-start(bf16[4,2,49152]{2,1,0:T(2,128)(2,1)} %reshape.957), calls=%async_computation.2 | async-start | bytes 1572864 | tf_op jit(solution)/shard_map/all_to_all | solution.py:234
  662.0 519.0 %reduce-scatter.29.cloned.1.call-start = ((), (), s32[]{:S(2)}) async-start(), calls=%async_computation.26 | async-start | bytes 15925248
  891.6 326.2 %reduce-scatter.25.cloned.1.call-start = ((), (), s32[]{:S(2)}) async-start(), calls=%async_computation.24 | async-start | bytes 442368
  905.9 348.7 %reduce-scatter.27.cloned.1.call-start = ((), (), s32[]{:S(2)}) async-start(), calls=%async_computation.25 | async-start | bytes 442368
  906.9 586.6 %all-reduce.9.cloned.1.call-start = ((), (), s32[]{:S(2)}) async-start(), calls=%async_computation.28 | async-start | bytes 13369344 | tf_op jit(solution)/shard_map/psum | solution.py:266
  1075.6 546.4 %all-gather.23.cloned.1.call-start = ((), (), s32[]{:S(2)}) async-start(), calls=%async_computation.23 | async-start | bytes 8847360 | tf_op jit(solution)/shard_map/all_gather | solution.py:263
  (86 other events, 1710.5 us)
Sparse Core Ops, SparseCore 0:
  9.9 81.4 all-gather.10
  93.3 78.6 all-gather.14
  173.8 38.7 all-gather.12
  214.4 38.7 all-gather.16
  254.9 98.5 all-gather.18
  355.3 98.5 all-gather.20
  503.1 36.9 all-reduce.6
  598.4 101.5 reduce-scatter.30
  704.0 53.7 reduce-scatter.18
  761.7 53.7 reduce-scatter.16
  819.2 126.4 reduce-scatter.20
  949.1 126.4 reduce-scatter.22
  1079.2 101.7 reduce-scatter.28
  1183.9 33.8 reduce-scatter.24
  1220.7 33.8 reduce-scatter.26
  1257.8 235.6 all-reduce.8
  1494.9 127.0 all-gather.22
